TPU v7x, 32 devices: a whole 2x2x4 slice. The times are simulated.
32 devices in a mesh: seq: 8 (over z, x), head: 4 (over y, core).
Axes of the slice: x: 2, y: 2, z: 4, core: 2. Of those that a mesh axis runs over, the one named last changes fastest.
Arguments:
- hidden_in: bfloat16 [256, 4096], P(None, 'seq'), may hold values from -6 to 6
- norm_gain: bfloat16 [1, 4096], P(None, 'seq'), may hold values from 0.25 to 1.75
- w_query: bfloat16 [4096, 4096], P('seq', 'head'), may hold values from -1 to 1
- w_key: bfloat16 [4096, 1024], P('seq', 'head'), may hold values from -1 to 1
- w_value: bfloat16 [4096, 1024], P('seq', 'head'), may hold values from -0.09375 to 0.09375
- w_out: bfloat16 [4096, 4096], P('head', 'seq'), may hold values from -0.09375 to 0.09375
- cache_keys: bfloat16 [32768, 8, 128], P('seq', 'head'), may hold values from -400 to 400
- cache_values: bfloat16 [32768, 8, 128], P('seq', 'head'), may hold values from -12 to 12
- lengths: int32 [8], replicated, may hold values from 512 to 4096, as said below
- span_start: int32 [1], replicated, may hold values from 0 to 256
Outputs:
- attn_out: bfloat16 [256, 4096], P('head', 'seq')
Inputs may be any that keep to these rules, and one draw needn't show every extreme that they name: Slots 0 to lengths[s] - 1 of shard s are live, the others empty; in every draw some shard is full.
All inputs are finite; a program needn't handle non-finite values.
Results may differ from a plain program's by a relative error of at most 0.039.
The roundings to bfloat16 on the way count: a program that leaves them out, or rounds other values in their place, can miss the bound.
Values may be sent and summed in bfloat16 or wider, within the bound.
No kernel may reach another device: no remote copies, remote signals or barrier semaphores. Data moves between devices by JAX's collectives and lax.ppermute only.
A program may use at most 64 MiB of HBM per device.

v0:
```python
import math
import jax
import jax.numpy as jnp
from jax import lax
from jax.sharding import PartitionSpec as P

D = 4096
rope_base = 500000.0
stretch = 64.0
initial_context = 8192.0
ramp_low = 1.0
ramp_high = 32.0
epsilon = 1e-05
negative = -1e30


def rope_parts(positions, head_dim):
    half_dim = head_dim // 2
    indices = jnp.arange(half_dim, dtype=jnp.float32)
    base_freq = jnp.power(jnp.float32(rope_base), -2.0 * indices / head_dim)
    wavelength = 2.0 * math.pi / base_freq
    turn_count = initial_context / wavelength
    ramp_share = jnp.clip((turn_count - ramp_low) / (ramp_high - ramp_low), 0.0, 1.0)
    frequency = (1.0 - ramp_share) * base_freq / stretch + ramp_share * base_freq
    angles = positions[:, None] * frequency[None, :]
    mscale = 0.1 * math.log(stretch) + 1.0
    return (jnp.cos(angles) * mscale, jnp.sin(angles) * mscale)


def rotate(vectors, cosine, sine_part):
    half_dim = vectors.shape[-1] // 2
    lower_half = vectors[..., :half_dim]
    upper_half = vectors[..., half_dim:]
    cosine = cosine[:, None, :]
    sine_part = sine_part[:, None, :]
    return jnp.concatenate(
        [
            lower_half * cosine - upper_half * sine_part,
            upper_half * cosine + lower_half * sine_part,
        ],
        -1,
    )


def round_trip(values):
    return lax.optimization_barrier(values.astype(jnp.bfloat16)).astype(jnp.float32)


def attend(running, queries, key_block, value_block, visible):
    maxima, totals, weighted = running
    scores = jnp.einsum("tgrd,kgd->grtk", queries, key_block, preferred_element_type=jnp.float32)
    scores = jnp.where(visible, scores, negative)
    new_max = jnp.maximum(maxima, jnp.max(scores, axis=-1))
    probability = jnp.where(visible, jnp.exp(scores - new_max[..., None]), 0.0)
    rescale = jnp.exp(maxima - new_max)
    totals = totals * rescale + jnp.sum(probability, axis=-1)
    weighted = weighted * rescale[..., None] + jnp.einsum(
        "grtk,kgd->grtd",
        probability.astype(jnp.bfloat16),
        value_block,
        preferred_element_type=jnp.float32,
    )
    return (new_max, totals, weighted)


def local(
    hidden_in,
    norm_gain,
    w_query,
    w_key,
    w_value,
    w_out,
    cache_keys,
    cache_values,
    lengths,
    span_start,
):
    seq_count = lax.axis_size("seq")
    my_index = lax.axis_index("seq")
    span_len = hidden_in.shape[0]
    local_kv = cache_keys.shape[1]
    head_dim = cache_keys.shape[2]
    group_size = w_query.shape[1] // (local_kv * head_dim)
    kv_cols = w_key.shape[1]
    row_count = span_len // seq_count
    first_new = my_index * row_count
    input_f32 = hidden_in.astype(jnp.float32)
    square_sums = lax.psum(jnp.sum(input_f32 * input_f32, axis=1), "seq")
    inv_rms = lax.rsqrt(square_sums[:, None] / D + epsilon)
    normed = (input_f32 * inv_rms * norm_gain.astype(jnp.float32)).astype(jnp.bfloat16)
    queries = lax.psum(jnp.dot(normed, w_query, preferred_element_type=jnp.float32), "seq")
    kv_own = lax.psum_scatter(
        jnp.concatenate(
            [
                jnp.dot(normed, w_key, preferred_element_type=jnp.float32),
                jnp.dot(normed, w_value, preferred_element_type=jnp.float32),
            ],
            1,
        ),
        "seq",
        scatter_dimension=0,
        tiled=True,
    )
    key_own = kv_own[:, :kv_cols]
    value_own = kv_own[:, kv_cols:]
    shard_ids = jnp.arange(lengths.shape[0], dtype=jnp.int32)
    offset = jnp.sum(jnp.where(shard_ids < my_index, lengths, 0))
    live_count = jnp.sum(jnp.where(shard_ids == my_index, lengths, 0))
    first_pos = jnp.sum(lengths) + span_start[0]
    query_pos = (first_pos + jnp.arange(span_len, dtype=jnp.int32)).astype(jnp.float32)
    cosine, sine_part = rope_parts(query_pos, head_dim)
    rotated = rotate(
        queries.reshape(span_len, local_kv * group_size, head_dim), cosine, sine_part
    ) * head_dim ** (-0.5)
    query_low = rotated.astype(jnp.bfloat16).reshape(span_len, local_kv, group_size, head_dim)
    my_keys = round_trip(key_own).reshape(row_count, local_kv, head_dim)
    my_values = value_own.astype(jnp.bfloat16).reshape(row_count, local_kv, head_dim)
    new_pos = (first_pos + first_new + jnp.arange(row_count, dtype=jnp.int32)).astype(jnp.float32)
    new_cos, new_sin = rope_parts(new_pos, head_dim)
    new_key_rot = rotate(my_keys, new_cos, new_sin).astype(jnp.bfloat16)
    block_len = math.gcd(cache_keys.shape[0], 1024)

    def sweep_block(block_index, running):
        block_start = block_index * block_len
        key_block = lax.dynamic_slice_in_dim(cache_keys, block_start, block_len, 0).astype(
            jnp.float32
        )
        value_block = lax.dynamic_slice_in_dim(cache_values, block_start, block_len, 0)
        slot_ids = block_start + jnp.arange(block_len, dtype=jnp.int32)
        occupied = slot_ids < live_count
        positions = (offset + slot_ids).astype(jnp.float32)
        block_cos, block_sin = rope_parts(positions, head_dim)
        block_keys = rotate(key_block, block_cos, block_sin).astype(jnp.bfloat16)
        return attend(running, query_low, block_keys, value_block, occupied[None, None, None, :])

    running = (
        jnp.full((local_kv, group_size, span_len), negative, jnp.float32),
        jnp.zeros((local_kv, group_size, span_len), jnp.float32),
        jnp.zeros((local_kv, group_size, span_len, head_dim), jnp.float32),
    )
    block_total = cache_keys.shape[0] // block_len
    running = lax.fori_loop(0, block_total, sweep_block, running)
    query_rows = jnp.arange(span_len, dtype=jnp.int32)[:, None]
    key_rows = first_new + jnp.arange(row_count, dtype=jnp.int32)[None, :]
    maxima, totals, weighted = attend(
        running, query_low, new_key_rot, my_values, (key_rows <= query_rows)[None, None]
    )
    global_max = lax.pmax(maxima, "seq")
    rescale = jnp.exp(maxima - global_max)
    totals, weighted = lax.psum((totals * rescale, weighted * rescale[..., None]), "seq")
    attended = (
        (weighted / totals[..., None])
        .transpose(2, 0, 1, 3)
        .reshape(span_len, local_kv * group_size * head_dim)
    )
    attended = attended.astype(jnp.bfloat16)
    partial_out = jnp.dot(attended, w_out, preferred_element_type=jnp.float32)
    return lax.psum_scatter(
        partial_out.astype(jnp.bfloat16), "head", scatter_dimension=0, tiled=True
    )


def solution(mesh):
    return jax.shard_map(
        local,
        mesh=mesh,
        in_specs=(
            P(None, "seq"),
            P(None, "seq"),
            P("seq", "head"),
            P("seq", "head"),
            P("seq", "head"),
            P("head", "seq"),
            P("seq", "head", None),
            P("seq", "head", None),
            P(),
            P(),
        ),
        out_specs=P("head", "seq"),
        check_vma=False,
    )
```

profile of v0, /device:TPU:0, one launch (start us, length us, event | category | flops | bytes accessed | tf_op | source)
XLA Modules:
  0.0 316.9 jit_solution(12627172227235214225)
XLA Ops:
  6.5 0.8 mul.477
  7.3 1.1 fusion.24
  8.4 23.1 %psum.28 = f32[256]{0:T(256)S(1)} all-reduce(f32[256]{0:T(256)S(1)} %fusion.24), channel_id=1, replica_groups=mesh['seq'=8,'head'=4] {'seq'}, use_global_device_ids=true, to_apply=%region_3.0 | all-reduce | flops 256 | bytes 2048 | tf_op jit(solution)/shard_map/psum | solution.py:88
  31.5 1.4 convolution_bitcast_fusion
  33.0 1.2 copy.68
  34.3 1.4 fusion.45
  35.7 1.4 fusion.47
  37.1 1.0 copy.62
  39.0 0.7 fusion.50
  41.1 68.9 %all-reduce.3.cloned.1.call-done = f32[256,8,128]{2,1,0:T(8,128)} async-done(((f32[256,8,128]{2,1,0:T(8,128)}), f32[256,8,128]{2,1,0:T(8,128)}) %all-reduce.3.cloned.1.call-update) | async-done | bytes 1048592 | tf_op jit(solution)/shard_map/psum | solution.py:91
  110.0 1.9 multiply_subtract_fusion
  112.7 74.1 %while.20 = (s32[]{:T(128)}, f32[2,4,256]{2,1,0:T(4,128)S(1)}, f32[2,4,256]{2,1,0:T(4,128)S(1)}, f32[2,4,256,128]{3,2,1,0:T(8,128)S(1)}, s32[]{:T(128)}, /*index...) while((s32[]{:T(128)}, f32[2,4,256]{2,1,0:T(4,128)S(1)}, ...), condition=%wide.region_9.10_spmd.clone, body=%wide.region_6.9_spmd.clone.sunk | while | flops 1098071808 | bytes 68825840 | solution.py:142
  112.7 0.6 fusion.70
  113.4 1.9 constant_dynamic-slice_fusion.3
  116.0 1.9 fusion.71
  118.4 4.0 %bitcast_reduce_fusion.2 = (f32[2,4,256]{2,1,0:T(4,128)S(1)}, f32[2,1024,256,4]{2,1,3,0:T(8,128)}) fusion(pred[1024]{0:T(1024)(128)(4,1)S(1)} %fusion.70, bf16[256,2,4,128]{3,0,2,1:T(8,128)(2,1)S(1)} %get-tuple-element.465, bf16[1024,2,64]{2,0,1:T(8,128)(2,1)S(1)} %get-tuple-element.425, bf16[1024,2,64]{2,0,1:T(8,128)(2,1)S(1)} %get-tuple-element.426), kind=kOutput, calls=%fused_computation.1.clone.1 | convolution fusion | flops 542111744 | bytes 9446400 | tf_op jit(solution)/shard_map/while/body/eval_jaxpr/tgrd,kgd->grtk/dot_general | solution.py:51
  122.4 4.6 %fusion.72 = f32[2,4,256]{2,1,0:T(4,128)S(1)} fusion(f32[2,1024,256,4]{2,1,3,0:T(8,128)} %get-tuple-element.428, f32[2,4,256]{2,1,0:T(4,128)S(1)} %select_maximum_fusion.2, pred[1024]{0:T(1024)(128)(4,1)S(1)} %fusion.70), kind=kLoop, calls=%fused_computation.5.clone.1 | loop fusion | flops 8386560 | bytes 8406016 | tf_op jit(solution)/shard_map/while/body/eval_jaxpr/reduce_sum | solution.py:56
  127.1 1.2 copy-done.1
  128.3 2.9 fusion.74
  131.3 0.6 fusion.70
  131.9 1.9 constant_dynamic-slice_fusion.3
  134.5 1.9 fusion.71
  136.9 4.1 %bitcast_reduce_fusion.2 = (f32[2,4,256]{2,1,0:T(4,128)S(1)}, f32[2,1024,256,4]{2,1,3,0:T(8,128)}) fusion(pred[1024]{0:T(1024)(128)(4,1)S(1)} %fusion.70, bf16[256,2,4,128]{3,0,2,1:T(8,128)(2,1)S(1)} %get-tuple-element.465, bf16[1024,2,64]{2,0,1:T(8,128)(2,1)S(1)} %get-tuple-element.425, bf16[1024,2,64]{2,0,1:T(8,128)(2,1)S(1)} %get-tuple-element.426), kind=kOutput, calls=%fused_computation.1.clone.1 | convolution fusion | flops 542111744 | bytes 9446400 | tf_op jit(solution)/shard_map/while/body/eval_jaxpr/tgrd,kgd->grtk/dot_general | solution.py:51
  141.0 4.7 %fusion.72 = f32[2,4,256]{2,1,0:T(4,128)S(1)} fusion(f32[2,1024,256,4]{2,1,3,0:T(8,128)} %get-tuple-element.428, f32[2,4,256]{2,1,0:T(4,128)S(1)} %select_maximum_fusion.2, pred[1024]{0:T(1024)(128)(4,1)S(1)} %fusion.70), kind=kLoop, calls=%fused_computation.5.clone.1 | loop fusion | flops 8386560 | bytes 8406016 | tf_op jit(solution)/shard_map/while/body/eval_jaxpr/reduce_sum | solution.py:56
  145.7 1.2 copy-done.1
  146.9 2.9 fusion.74
  149.8 0.6 fusion.70
  150.5 1.9 constant_dynamic-slice_fusion.3
  153.1 1.9 fusion.71
  155.5 4.0 %bitcast_reduce_fusion.2 = (f32[2,4,256]{2,1,0:T(4,128)S(1)}, f32[2,1024,256,4]{2,1,3,0:T(8,128)}) fusion(pred[1024]{0:T(1024)(128)(4,1)S(1)} %fusion.70, bf16[256,2,4,128]{3,0,2,1:T(8,128)(2,1)S(1)} %get-tuple-element.465, bf16[1024,2,64]{2,0,1:T(8,128)(2,1)S(1)} %get-tuple-element.425, bf16[1024,2,64]{2,0,1:T(8,128)(2,1)S(1)} %get-tuple-element.426), kind=kOutput, calls=%fused_computation.1.clone.1 | convolution fusion | flops 542111744 | bytes 9446400 | tf_op jit(solution)/shard_map/while/body/eval_jaxpr/tgrd,kgd->grtk/dot_general | solution.py:51
  159.5 4.6 %fusion.72 = f32[2,4,256]{2,1,0:T(4,128)S(1)} fusion(f32[2,1024,256,4]{2,1,3,0:T(8,128)} %get-tuple-element.428, f32[2,4,256]{2,1,0:T(4,128)S(1)} %select_maximum_fusion.2, pred[1024]{0:T(1024)(128)(4,1)S(1)} %fusion.70), kind=kLoop, calls=%fused_computation.5.clone.1 | loop fusion | flops 8386560 | bytes 8406016 | tf_op jit(solution)/shard_map/while/body/eval_jaxpr/reduce_sum | solution.py:56
  164.2 1.2 copy-done.1
  165.4 2.9 fusion.74
  168.4 0.6 fusion.70
  169.0 1.9 constant_dynamic-slice_fusion.3
  171.6 1.9 fusion.71
  174.0 4.0 %bitcast_reduce_fusion.2 = (f32[2,4,256]{2,1,0:T(4,128)S(1)}, f32[2,1024,256,4]{2,1,3,0:T(8,128)}) fusion(pred[1024]{0:T(1024)(128)(4,1)S(1)} %fusion.70, bf16[256,2,4,128]{3,0,2,1:T(8,128)(2,1)S(1)} %get-tuple-element.465, bf16[1024,2,64]{2,0,1:T(8,128)(2,1)S(1)} %get-tuple-element.425, bf16[1024,2,64]{2,0,1:T(8,128)(2,1)S(1)} %get-tuple-element.426), kind=kOutput, calls=%fused_computation.1.clone.1 | convolution fusion | flops 542111744 | bytes 9446400 | tf_op jit(solution)/shard_map/while/body/eval_jaxpr/tgrd,kgd->grtk/dot_general | solution.py:51
  178.1 4.6 %fusion.72 = f32[2,4,256]{2,1,0:T(4,128)S(1)} fusion(f32[2,1024,256,4]{2,1,3,0:T(8,128)} %get-tuple-element.428, f32[2,4,256]{2,1,0:T(4,128)S(1)} %select_maximum_fusion.2, pred[1024]{0:T(1024)(128)(4,1)S(1)} %fusion.70), kind=kLoop, calls=%fused_computation.5.clone.1 | loop fusion | flops 8386560 | bytes 8406016 | tf_op jit(solution)/shard_map/while/body/eval_jaxpr/reduce_sum | solution.py:56
  182.7 1.2 copy-done.1
  183.9 2.9 fusion.74
  186.9 0.8 convert.18
  188.2 20.3 %pmax.7 = f32[2,4,256]{2,1,0:T(4,128)S(1)} all-reduce(f32[2,4,256]{2,1,0:T(4,128)S(1)} %max.32), channel_id=1, replica_groups=mesh['seq'=8,'head'=4] {'seq'}, use_global_device_ids=true, to_apply=%region_12.13 | all-reduce | flops 2048 | bytes 16384 | tf_op jit(solution)/shard_map/pmax | solution.py:148
  208.7 1.8 fusion.21
  210.5 18.0 %psum.31 = f32[2,4,256]{2,1,0:T(4,128)S(1)} all-reduce(f32[2,4,256]{2,1,0:T(4,128)S(1)} %bitcast.91), channel_id=1, replica_groups=mesh['seq'=8,'head'=4] {'seq'}, use_global_device_ids=true, to_apply=%region_15.16 | all-reduce | flops 2048 | bytes 16384 | tf_op jit(solution)/shard_map/psum | solution.py:150
  228.5 57.8 %all-reduce.5.cloned.1.call-done = f32[2,4,256,128]{3,2,1,0:T(8,128)} async-done(((f32[2,4,256,128]{3,2,1,0:T(8,128)}), f32[2,4,256,128]{3,2,1,0:T(8,128)}) %all-reduce.5.cloned.1.call-update) | async-done | bytes 1048592 | tf_op jit(solution)/shard_map/psum | solution.py:150
  286.4 1.6 fusion.27
  288.2 2.4 convolution_convert_fusion
  290.6 19.8 %reduce-scatter.5.cloned.1.call-done = bf16[64,512]{1,0:T(8,128)(2,1)} async-done(((bf16[256,512]{1,0:T(8,128)(2,1)}), bf16[64,512]{1,0:T(8,128)(2,1)}) %reduce-scatter.5.cloned.1.call-update) | async-done | bytes 65552 | tf_op jit(solution)/shard_map/reduce_scatter | solution.py:158
  (70 shorter events, 7.2 us)
Async XLA Ops:
  6.5 25.0 %copy-start = (bf16[512,1024]{1,0:T(8,128)(2,1)S(1)}, bf16[512,1024]{1,0:T(8,128)(2,1)}, u32[]{:S(2)}) copy-start(bf16[512,1024]{1,0:T(8,128)(2,1)} %param.14) | copy-start | bytes 3145732
  6.5 32.4 %copy-start.2 = (s32[8]{0:T(128)S(1)}, s32[8]{0:T(128)}, u32[]{:S(2)}) copy-start(s32[8]{0:T(128)} %param.20) | copy-start | bytes 100
  6.5 103.5 %all-reduce.3.cloned.1.call-start = ((), (), s32[]{:S(2)}) async-start(), calls=%async_computation.2 | async-start | bytes 2097152 | tf_op jit(solution)/shard_map/psum | solution.py:91
  34.2 152.6 %reduce-scatter.7.cloned.1.call-start = ((), (), s32[]{:S(2)}) async-start(), calls=%async_computation.5 | async-start | bytes 589824 | tf_op jit(solution)/shard_map/reduce_scatter | solution.py:92
  38.2 248.2 %all-reduce.5.cloned.1.call-start = ((), (), s32[]{:S(2)}) async-start(), calls=%async_computation.3 | async-start | bytes 2097152 | tf_op jit(solution)/shard_map/psum | solution.py:150
  122.4 5.9 %copy-start.1 = (f32[2,1024,256,4]{2,1,3,0:T(8,128)S(1)}, f32[2,1024,256,4]{2,1,3,0:T(8,128)}, u32[]{:S(2)}) copy-start(f32[2,1024,256,4]{2,1,3,0:T(8,128)} %get-tuple-element.428) | copy-start | bytes 25165828 | tf_op jit(solution)/shard_map/while
  141.0 5.9 %copy-start.1 = (f32[2,1024,256,4]{2,1,3,0:T(8,128)S(1)}, f32[2,1024,256,4]{2,1,3,0:T(8,128)}, u32[]{:S(2)}) copy-start(f32[2,1024,256,4]{2,1,3,0:T(8,128)} %get-tuple-element.428) | copy-start | bytes 25165828 | tf_op jit(solution)/shard_map/while
  159.5 5.9 %copy-start.1 = (f32[2,1024,256,4]{2,1,3,0:T(8,128)S(1)}, f32[2,1024,256,4]{2,1,3,0:T(8,128)}, u32[]{:S(2)}) copy-start(f32[2,1024,256,4]{2,1,3,0:T(8,128)} %get-tuple-element.428) | copy-start | bytes 25165828 | tf_op jit(solution)/shard_map/while
  178.0 5.8 %copy-start.1 = (f32[2,1024,256,4]{2,1,3,0:T(8,128)S(1)}, f32[2,1024,256,4]{2,1,3,0:T(8,128)}, u32[]{:S(2)}) copy-start(f32[2,1024,256,4]{2,1,3,0:T(8,128)} %get-tuple-element.428) | copy-start | bytes 25165828 | tf_op jit(solution)/shard_map/while
  210.5 99.9 %reduce-scatter.5.cloned.1.call-start = ((), (), s32[]{:S(2)}) async-start(), calls=%async_computation.4 | async-start | bytes 327680 | tf_op jit(solution)/shard_map/reduce_scatter | solution.py:158
Sparse Core Ops, SparseCore 0:
  34.4 75.6 all-reduce.2
  113.4 62.1 reduce-scatter.6
  210.6 75.7 all-reduce.4
  290.7 19.6 reduce-scatter.4
where the time goes:
time: 318 us; the launch traced here: 317 us
  waiting for transfers between devices  147 us (46%)
  blocking collectives  61.5 us (19%)
  other arithmetic  41.5 us (13%)
  matrix products  36.7 us (12%)
  local copies, waits for them, and re-layouts  15.5 us (5%)
  between operations  14.7 us (5%)
    psum x1, waiting for transfers between devices, local(): lax.psum(jnp.dot(normed, w_query, preferred_element_type=jnp.float32), 's...  68.9 us
    psum x1, waiting for transfers between devices, local(): lax.psum((totals * rescale, weighted * rescale[..., None]), 'seq')  57.8 us
    psum x1, blocking collectives, local(): square_sums = lax.psum(jnp.sum(input_f32 * input_f32, axis=1), 'seq')  23.1 us
    pmax x1, blocking collectives, local(): global_max = lax.pmax(maxima, 'seq')  20.3 us
    reduce_scatter x1, waiting for transfers between devices, local(): lax.psum_scatter(partial_out.astype(jnp.bfloat16), 'head', scatter_dimens...  19.8 us
    reduce_sum x5, other arithmetic, attend(): totals = totals * rescale + jnp.sum(probability, axis=-1)  18.7 us
    psum x1, blocking collectives, local(): lax.psum((totals * rescale, weighted * rescale[..., None]), 'seq')  18 us
    dot_general x5, matrix products, attend(): jnp.einsum('tgrd,kgd->grtk', queries, key_block, preferred_element_type=j...  16.5 us
  transfers between devices with their start and end apart: 4, of which 3 were waited for; matrix products, arithmetic and copies ran while one was open for 24% of the time, Pallas kernels for 0%

commit v1 on v0

--- a/solution.py
+++ b/solution.py
@@ -88,7 +88,9 @@
     square_sums = lax.psum(jnp.sum(input_f32 * input_f32, axis=1), "seq")
     inv_rms = lax.rsqrt(square_sums[:, None] / D + epsilon)
     normed = (input_f32 * inv_rms * norm_gain.astype(jnp.float32)).astype(jnp.bfloat16)
-    queries = lax.psum(jnp.dot(normed, w_query, preferred_element_type=jnp.float32), "seq")
+    own = jnp.dot(normed, w_query, preferred_element_type=jnp.float32)
+    parts = lax.all_gather(own, "seq")
+    queries = jnp.sum(parts, axis=0)
     kv_own = lax.psum_scatter(
         jnp.concatenate(
             [

time: 318 us -> 439 us (1.38)
  waiting for transfers between devices: 147 us -> 256 us
  local copies, waits for them, and re-layouts: 15.5 us -> 21 us
  other arithmetic: 41.5 us -> 46.8 us
    all_gather x0 -> x1, waiting for transfers between devices: none -> 125 us  [local(): parts = lax.all_gather(own, 'seq')]
    psum x1 -> x0, waiting for transfers between devices: 68.9 us -> none  [local(): lax.psum(jnp.dot(normed, w_query, preferred_element_type=jnp.float32), 's...]
    reduce_scatter x1, waiting for transfers between devices: 0.02 us -> 54.3 us  [local(): lax.psum_scatter(jnp.concatenate([jnp.dot(normed, w_key, preferred_elemen...]
    while x12 -> x28, local copies, waits for them, and re-layouts: 4.73 us -> 8.88 us
  transfers between devices with their start and end apart: 4 -> 4, of which waited for: 3 -> 4; matrix products, arithmetic and copies ran while one was open for 24% -> 1% of each run, Pallas kernels for 0% -> 0%
where the time goes in v1:
time: 439 us; the launch traced here: 438 us
  waiting for transfers between devices  256 us (58%)
  blocking collectives  60.6 us (14%)
  other arithmetic  46.8 us (11%)
  matrix products  38.5 us (9%)
  local copies, waits for them, and re-layouts  21 us (5%)
  between operations  14.5 us (3%)
    all_gather x1, waiting for transfers between devices, local(): parts = lax.all_gather(own, 'seq')  125 us
    psum x1, waiting for transfers between devices, local(): lax.psum((totals * rescale, weighted * rescale[..., None]), 'seq')  57.1 us
    reduce_scatter x1, waiting for transfers between devices, local(): lax.psum_scatter(jnp.concatenate([jnp.dot(normed, w_key, preferred_elemen...  54.3 us
    psum x1, blocking collectives, local(): square_sums = lax.psum(jnp.sum(input_f32 * input_f32, axis=1), 'seq')  23.1 us
    reduce_scatter x1, waiting for transfers between devices, local(): lax.psum_scatter(partial_out.astype(jnp.bfloat16), 'head', scatter_dimens...  19.8 us
    pmax x1, blocking collectives, local(): global_max = lax.pmax(maxima, 'seq')  18.7 us
    psum x1, blocking collectives, local(): lax.psum((totals * rescale, weighted * rescale[..., None]), 'seq')  18.7 us
    reduce_sum x5, other arithmetic, attend(): totals = totals * rescale + jnp.sum(probability, axis=-1)  18.6 us
  transfers between devices with their start and end apart: 4, of which 4 were waited for; matrix products, arithmetic and copies ran while one was open for 1% of the time, Pallas kernels for 0%

profile of v1, /device:TPU:0, one launch (start us, length us, event | category | flops | bytes accessed | tf_op | source)
XLA Modules:
  0.0 437.9 jit_solution(14526152249112623079)
XLA Ops:
  7.3 1.1 fusion.24
  8.4 23.1 %psum.21 = f32[256]{0:T(256)S(1)} all-reduce(f32[256]{0:T(256)S(1)} %fusion.24), channel_id=1, replica_groups=mesh['seq'=8,'head'=4] {'seq'}, use_global_device_ids=true, to_apply=%region_3.0 | all-reduce | flops 256 | bytes 2048 | tf_op jit(solution)/shard_map/psum | solution.py:88
  31.5 1.4 fusion.45
  32.9 1.4 fusion.47
  35.5 2.4 fusion.49
  38.7 1.4 fusion.51
  41.2 54.3 %reduce-scatter.7.cloned.1.call-done = f32[32,512]{1,0:T(8,128)} async-done(((f32[256,512]{1,0:T(8,128)}), f32[32,512]{1,0:T(8,128)}) %reduce-scatter.7.cloned.1.call-update) | async-done | bytes 65552 | tf_op jit(solution)/shard_map/reduce_scatter | solution.py:94
  96.5 124.6 %all-gather.3.cloned.1.call-done = f32[2048,1024]{1,0:T(8,128)} async-done(((f32[256,1024]{1,0:T(8,128)}), f32[2048,1024]{1,0:T(8,128)}) %all-gather.3.cloned.1.call-update) | async-done | bytes 8388624 | tf_op jit(solution)/shard_map/all_gather | solution.py:92
  221.2 4.4 reduce_sum.73
  226.8 1.4 copy.48
  228.2 1.3 copy.47
  229.5 1.6 fusion.23
  231.1 78.3 %while.20 = (s32[]{:T(128)}, f32[2,4,256]{2,1,0:T(4,128)S(1)}, f32[2,4,256]{2,1,0:T(4,128)S(1)}, f32[2,4,256,128]{3,2,1,0:T(8,128)}, s32[]{:T(128)}, /*index=5*/...) while((s32[]{:T(128)}, f32[2,4,256]{2,1,0:T(4,128)S(1)}, ...), condition=%wide.region_9.10_spmd.clone, body=%wide.region_6.9_spmd.clone.sunk | while | flops 1098071808 | bytes 77214504 | solution.py:144
  231.7 1.9 constant_dynamic-slice_fusion.3
  234.4 1.9 fusion.72
  236.8 4.0 bitcast_reduce_fusion.2
  240.9 4.6 %fusion.73 = f32[2,4,256]{2,1,0:T(4,128)S(1)} fusion(f32[2,1024,256,4]{2,1,3,0:T(8,128)} %get-tuple-element.428, f32[2,4,256]{2,1,0:T(4,128)S(1)} %select_maximum_fusion.2, pred[1024]{0:T(1024)(128)(4,1)S(1)} %fusion.71), kind=kLoop, calls=%fused_computation.5.clone.1 | loop fusion | flops 8386560 | bytes 8406016 | tf_op jit(solution)/shard_map/while/body/eval_jaxpr/reduce_sum | solution.py:56
  245.5 1.1 copy-done.1
  246.7 2.9 fusion.75
  249.6 1.1 copy-done.3
  251.3 1.9 constant_dynamic-slice_fusion.3
  254.0 1.9 fusion.72
  256.4 4.0 bitcast_reduce_fusion.2
  260.5 4.6 %fusion.73 = f32[2,4,256]{2,1,0:T(4,128)S(1)} fusion(f32[2,1024,256,4]{2,1,3,0:T(8,128)} %get-tuple-element.428, f32[2,4,256]{2,1,0:T(4,128)S(1)} %select_maximum_fusion.2, pred[1024]{0:T(1024)(128)(4,1)S(1)} %fusion.71), kind=kLoop, calls=%fused_computation.5.clone.1 | loop fusion | flops 8386560 | bytes 8406016 | tf_op jit(solution)/shard_map/while/body/eval_jaxpr/reduce_sum | solution.py:56
  265.1 1.1 copy-done.1
  266.3 2.9 fusion.75
  269.2 1.1 copy-done.3
  270.9 1.9 constant_dynamic-slice_fusion.3
  273.6 1.9 fusion.72
  276.0 4.0 bitcast_reduce_fusion.2
  280.0 4.6 %fusion.73 = f32[2,4,256]{2,1,0:T(4,128)S(1)} fusion(f32[2,1024,256,4]{2,1,3,0:T(8,128)} %get-tuple-element.428, f32[2,4,256]{2,1,0:T(4,128)S(1)} %select_maximum_fusion.2, pred[1024]{0:T(1024)(128)(4,1)S(1)} %fusion.71), kind=kLoop, calls=%fused_computation.5.clone.1 | loop fusion | flops 8386560 | bytes 8406016 | tf_op jit(solution)/shard_map/while/body/eval_jaxpr/reduce_sum | solution.py:56
  284.7 1.1 copy-done.1
  285.9 2.9 fusion.75
  288.8 1.1 copy-done.3
  290.5 1.9 constant_dynamic-slice_fusion.3
  293.2 1.9 fusion.72
  295.6 4.0 bitcast_reduce_fusion.2
  299.6 4.6 %fusion.73 = f32[2,4,256]{2,1,0:T(4,128)S(1)} fusion(f32[2,1024,256,4]{2,1,3,0:T(8,128)} %get-tuple-element.428, f32[2,4,256]{2,1,0:T(4,128)S(1)} %select_maximum_fusion.2, pred[1024]{0:T(1024)(128)(4,1)S(1)} %fusion.71), kind=kLoop, calls=%fused_computation.5.clone.1 | loop fusion | flops 8386560 | bytes 8406016 | tf_op jit(solution)/shard_map/while/body/eval_jaxpr/reduce_sum | solution.py:56
  304.3 1.1 copy-done.1
  305.4 2.9 fusion.75
  308.4 1.1 copy-done.3
  309.8 18.7 %pmax.7 = f32[2,4,256]{2,1,0:T(4,128)S(1)} all-reduce(f32[2,4,256]{2,1,0:T(4,128)S(1)} %max.32), channel_id=1, replica_groups=mesh['seq'=8,'head'=4] {'seq'}, use_global_device_ids=true, to_apply=%region_12.13 | all-reduce | flops 2048 | bytes 16384 | tf_op jit(solution)/shard_map/pmax | solution.py:150
  328.6 2.8 fusion.21
  331.5 18.7 %psum.23 = f32[2,4,256]{2,1,0:T(4,128)S(1)} all-reduce(f32[2,4,256]{2,1,0:T(4,128)S(1)} %bitcast.91), channel_id=1, replica_groups=mesh['seq'=8,'head'=4] {'seq'}, use_global_device_ids=true, to_apply=%region_15.16 | all-reduce | flops 2048 | bytes 16384 | tf_op jit(solution)/shard_map/psum | solution.py:152
  350.2 57.1 %all-reduce.2.cloned.1.call-done = f32[2,4,256,128]{3,2,1,0:T(8,128)} async-done(((f32[2,4,256,128]{3,2,1,0:T(8,128)}), f32[2,4,256,128]{3,2,1,0:T(8,128)}) %all-reduce.2.cloned.1.call-update) | async-done | bytes 1048592 | tf_op jit(solution)/shard_map/psum | solution.py:152
  407.3 1.6 fusion.27
  409.1 2.4 convolution_convert_fusion
  411.5 19.8 %reduce-scatter.5.cloned.1.call-done = bf16[64,512]{1,0:T(8,128)(2,1)} async-done(((bf16[256,512]{1,0:T(8,128)(2,1)}), bf16[64,512]{1,0:T(8,128)(2,1)}) %reduce-scatter.5.cloned.1.call-update) | async-done | bytes 65552 | tf_op jit(solution)/shard_map/reduce_scatter | solution.py:160
  (85 shorter events, 12.9 us)
Async XLA Ops:
  6.5 28.9 %copy-start = (bf16[512,1024]{1,0:T(8,128)(2,1)S(1)}, bf16[512,1024]{1,0:T(8,128)(2,1)}, u32[]{:S(2)}) copy-start(bf16[512,1024]{1,0:T(8,128)(2,1)} %param.14) | copy-start | bytes 3145732
  6.5 89.0 %reduce-scatter.7.cloned.1.call-start = ((), (), s32[]{:S(2)}) async-start(), calls=%async_computation.5 | async-start | bytes 589824 | tf_op jit(solution)/shard_map/reduce_scatter | solution.py:94
  35.4 185.7 %all-gather.3.cloned.1.call-start = ((), (), s32[]{:S(2)}) async-start(), calls=%async_computation.4 | async-start | bytes 9437184 | tf_op jit(solution)/shard_map/all_gather | solution.py:92
  37.9 369.4 %all-reduce.2.cloned.1.call-start = ((), (), s32[]{:S(2)}) async-start(), calls=%async_computation.2 | async-start | bytes 2097152 | tf_op jit(solution)/shard_map/psum | solution.py:152
  236.8 8.7 %copy-start.2 = (f32[2,4,256,128]{3,2,1,0:T(8,128)S(1)}, f32[2,4,256,128]{3,2,1,0:T(8,128)}, u32[]{:S(2)}) copy-start(f32[2,4,256,128]{3,2,1,0:T(8,128)} %get-tuple-element.448) | copy-start | bytes 3145732 | tf_op jit(solution)/shard_map/while
  240.9 5.8 %copy-start.1 = (f32[2,1024,256,4]{2,1,3,0:T(8,128)S(1)}, f32[2,1024,256,4]{2,1,3,0:T(8,128)}, u32[]{:S(2)}) copy-start(f32[2,1024,256,4]{2,1,3,0:T(8,128)} %get-tuple-element.428) | copy-start | bytes 25165828 | tf_op jit(solution)/shard_map/while
  249.6 1.1 copy-start.3
  256.4 8.7 %copy-start.2 = (f32[2,4,256,128]{3,2,1,0:T(8,128)S(1)}, f32[2,4,256,128]{3,2,1,0:T(8,128)}, u32[]{:S(2)}) copy-start(f32[2,4,256,128]{3,2,1,0:T(8,128)} %get-tuple-element.448) | copy-start | bytes 3145732 | tf_op jit(solution)/shard_map/while
  260.4 5.8 %copy-start.1 = (f32[2,1024,256,4]{2,1,3,0:T(8,128)S(1)}, f32[2,1024,256,4]{2,1,3,0:T(8,128)}, u32[]{:S(2)}) copy-start(f32[2,1024,256,4]{2,1,3,0:T(8,128)} %get-tuple-element.428) | copy-start | bytes 25165828 | tf_op jit(solution)/shard_map/while
  269.2 1.1 copy-start.3
  276.0 8.7 %copy-start.2 = (f32[2,4,256,128]{3,2,1,0:T(8,128)S(1)}, f32[2,4,256,128]{3,2,1,0:T(8,128)}, u32[]{:S(2)}) copy-start(f32[2,4,256,128]{3,2,1,0:T(8,128)} %get-tuple-element.448) | copy-start | bytes 3145732 | tf_op jit(solution)/shard_map/while
  280.0 5.8 %copy-start.1 = (f32[2,1024,256,4]{2,1,3,0:T(8,128)S(1)}, f32[2,1024,256,4]{2,1,3,0:T(8,128)}, u32[]{:S(2)}) copy-start(f32[2,1024,256,4]{2,1,3,0:T(8,128)} %get-tuple-element.428) | copy-start | bytes 25165828 | tf_op jit(solution)/shard_map/while
  288.8 1.1 copy-start.3
  295.6 8.7 %copy-start.2 = (f32[2,4,256,128]{3,2,1,0:T(8,128)S(1)}, f32[2,4,256,128]{3,2,1,0:T(8,128)}, u32[]{:S(2)}) copy-start(f32[2,4,256,128]{3,2,1,0:T(8,128)} %get-tuple-element.448) | copy-start | bytes 3145732 | tf_op jit(solution)/shard_map/while
  299.6 5.8 %copy-start.1 = (f32[2,1024,256,4]{2,1,3,0:T(8,128)S(1)}, f32[2,1024,256,4]{2,1,3,0:T(8,128)}, u32[]{:S(2)}) copy-start(f32[2,1024,256,4]{2,1,3,0:T(8,128)} %get-tuple-element.428) | copy-start | bytes 25165828 | tf_op jit(solution)/shard_map/while
  308.4 1.1 copy-start.3
  331.4 99.9 %reduce-scatter.5.cloned.1.call-start = ((), (), s32[]{:S(2)}) async-start(), calls=%async_computation.3 | async-start | bytes 327680 | tf_op jit(solution)/shard_map/reduce_scatter | solution.py:160
Sparse Core Ops, SparseCore 0:
  35.5 59.9 reduce-scatter.6
  97.6 123.4 all-gather.2
  331.6 75.7 all-reduce.1
  411.6 19.6 reduce-scatter.4
